TPU v7x, 128 devices: a whole 4x4x4 slice. The times are simulated.
128 devices in a mesh: ax: 8 (over y, z_lo), az: 16 (over z_hi, x, core).
Axes of the slice: x: 4, y: 4, z: 4 (z_hi: 2, z_lo: 2; z = z_hi * 2 + z_lo), core: 2. Of those that a mesh axis runs over, the one named last changes fastest.
Arguments:
- saved_flow: float32 [3, 256, 64, 1024], P(None, 'az', None, 'ax'), may hold values from -6 to 6
- saved_adjoint: float32 [3, 256, 64, 1024], P(None, 'az', None, 'ax'), may hold values from -6 to 6
- tangent: float32 [3, 256, 64, 1024], P(None, 'az', None, 'ax'), may hold values from -6 to 6
- second_adjoint: float32 [3, 256, 64, 1024], P(None, 'az', None, 'ax'), may hold values from -6 to 6
- radial_rate: float32 [64], replicated, may hold values from 1 to 100
Outputs:
- tangent_next: float32 [3, 256, 64, 1024], P(None, 'az', None, 'ax')
- second_next: float32 [3, 256, 64, 1024], P(None, 'az', None, 'ax')
All inputs are finite; a program needn't handle non-finite values.
Results may differ from a plain program's by a relative error of at most 0.00005.
Values sent between devices are 32-bit elements; how exact they have to be, the bound alone decides.
No kernel may reach another device: no remote copies, remote signals or barrier semaphores. Data moves between devices by JAX's collectives and lax.ppermute only.
A program may use at most 128 MiB of HBM per device.

v0:
```python
import math
import jax
import jax.numpy as jnp
from jax import lax
from jax.sharding import PartitionSpec as P

time_step = 0.1
viscosity = 0.005
axial_unit = 2.0 * math.pi / 20.0


def radial_table(count):
    points = jnp.arange(count, dtype=jnp.int32)[:, None]
    orders = jnp.arange(count, dtype=jnp.int32)[None, :]
    phases = orders * (2 * points + 1) % (4 * count)
    values = jnp.cos(phases.astype(jnp.float32) * (math.pi / (2.0 * count)))
    scales = jnp.where(orders == 0, math.sqrt(1.0 / count), math.sqrt(2.0 / count))
    return values * scales


def hartley_table(length):
    row_index = jnp.arange(length, dtype=jnp.int32)[:, None]
    col_index = jnp.arange(length, dtype=jnp.int32)[None, :]
    phases = row_index * col_index % length
    angles = phases.astype(jnp.float32) * (2.0 * math.pi / length)
    return (jnp.cos(angles) + jnp.sin(angles)) / math.sqrt(length)


def body(saved_flow, saved_adjoint, tangent, second_adjoint, radial_rate):
    components = tangent.shape[0]
    local_azimuth = tangent.shape[1]
    radial_count = tangent.shape[2]
    local_axial = tangent.shape[3]
    azimuth_count = local_azimuth * lax.axis_size("az")
    axial_count = local_axial * lax.axis_size("ax")
    radial = radial_table(radial_count)
    azimuth_table = hartley_table(azimuth_count)
    axial_table = hartley_table(axial_count)

    def along_azimuth(field):
        return jnp.einsum("nm,cmjk->cnjk", azimuth_table, field, precision=lax.Precision.HIGHEST)

    def along_axial(field):
        return jnp.einsum("nk,cmjk->cmjn", axial_table, field, precision=lax.Precision.HIGHEST)

    stacked = jnp.concatenate((saved_flow, saved_adjoint, tangent, second_adjoint), axis=0)
    grid = jnp.einsum("jr,cmrk->cmjk", radial, stacked, precision=lax.Precision.HIGHEST)
    halfway = along_azimuth(lax.all_to_all(grid, "az", split_axis=2, concat_axis=1, tiled=True))
    physical = along_axial(lax.all_to_all(halfway, "ax", split_axis=1, concat_axis=3, tiled=True))
    flow = physical[0:components]
    adjoint = physical[components : 2 * components]
    tang = physical[2 * components : 3 * components]
    second = physical[3 * components : 4 * components]
    flow_sum = jnp.sum(flow, axis=0)[None]
    adjoint_sum = jnp.sum(adjoint, axis=0)[None]
    tang_sum = jnp.sum(tang, axis=0)[None]
    second_sum = jnp.sum(second, axis=0)[None]
    tangent_rhs = flow * tang_sum + tang * flow_sum
    second_rhs = flow * second_sum + second * flow_sum + adjoint * tang_sum + tang * adjoint_sum
    products = jnp.concatenate((tangent_rhs, second_rhs), axis=0)
    partial_field = along_axial(products)
    turned = along_azimuth(
        lax.all_to_all(partial_field, "ax", split_axis=3, concat_axis=1, tiled=True)
    )
    spectral = jnp.einsum(
        "jr,cmjk->cmrk",
        radial,
        lax.all_to_all(turned, "az", split_axis=1, concat_axis=2, tiled=True),
        precision=lax.Precision.HIGHEST,
    )
    azimuth = lax.axis_index("az") * local_azimuth + jnp.arange(local_azimuth, dtype=jnp.int32)
    wave_azimuth = jnp.minimum(azimuth, azimuth_count - azimuth).astype(jnp.float32)
    axial = lax.axis_index("ax") * local_axial + jnp.arange(local_axial, dtype=jnp.int32)
    wave_axial = jnp.minimum(axial, axial_count - axial).astype(jnp.float32) * axial_unit
    total = (
        radial_rate[None, :, None]
        + (wave_azimuth**2)[:, None, None]
        + (wave_axial**2)[None, None, :]
    )
    denom = (1.0 + viscosity * total)[None]
    tangent_next = (tangent + time_step * spectral[0:components]) / denom
    second_next = (second_adjoint + time_step * spectral[components : 2 * components]) / denom
    return (tangent_next, second_next)


def solution(mesh):
    in_specs = (
        P(None, "az", None, "ax"),
        P(None, "az", None, "ax"),
        P(None, "az", None, "ax"),
        P(None, "az", None, "ax"),
        P(),
    )
    out_specs = (P(None, "az", None, "ax"), P(None, "az", None, "ax"))
    return jax.shard_map(body, mesh=mesh, in_specs=in_specs, out_specs=out_specs, check_vma=False)
```

profile of v0, /device:TPU:3, one launch (start us, length us, event | category | flops | bytes accessed | tf_op | source)
XLA Modules:
  0.0 556.9 jit_solution(827337466593299157)
XLA Ops:
  0.7 8.1 %fusion.23 = f32[12,16,64,128]{3,2,1,0:T(8,128)S(1)} fusion(f32[3,16,64,128]{3,2,1,0:T(8,128)} %param.8, f32[3,16,64,128]{3,2,1,0:T(8,128)} %param.7, f32[3,16,64,128]{3,2,1,0:T(8,128)} %param.6, f32[3,16,64,128]{3,2,1,0:T(8,128)} %param.5, f32[64]{0:T(128)S(1)} %compare_select_fusion, s32[64]{0:T(128)S(1)} %multiply_add_fusion.3), kind=kOutput, calls=%fused_computation.27 | convolution fusion | flops 1212739584 | bytes 12583424 | tf_op jit(solution)/shard_map/jr,cmrk->cmjk/dot_general | solution.py:47
  8.7 3.6 copy.33
  12.4 79.9 %all_to_all.72 = f32[12,16,64,128]{3,1,0,2:T(8,128)S(1)} all-to-all(f32[12,16,64,128]{3,1,0,2:T(8,128)S(1)} %copy.33), channel_id=1, replica_groups=mesh['ax'=8,'az'=16] {'az'}, dimensions={2} | all-to-all | bytes 12582912 | tf_op jit(solution)/shard_map/all_to_all | solution.py:48
  92.3 0.9 copy.35
  93.2 14.3 %convolution_bitcast_fusion = f32[12,256,4,128]{1,3,2,0:T(8,128)} fusion(f32[12,256,4,128]{3,1,2,0:T(8,128)S(1)} %bitcast.66), kind=kOutput, calls=%fused_computation.28 | convolution fusion | flops 4832886784 | bytes 12582912 | tf_op jit(solution)/shard_map/nm,cmjk->cnjk/dot_general | solution.py:41
  107.5 7.9 %copy.37 = f32[12,256,4,128]{3,2,0,1:T(4,128)} copy(f32[12,256,4,128]{1,3,2,0:T(8,128)} %convolution_bitcast_fusion) | data formatting | bytes 12582912 | tf_op jit(solution)/shard_map/nm,cmjk->cnjk/transpose | solution.py:41
  115.4 5.0 all-to-all-start.1
  120.4 17.7 %fusion.108 = f32[1024,1024,1,1]{1,0,3,2:T(8,128)} fusion(), kind=kLoop, calls=%fused_computation.19.clone.1 | loop fusion | flops 16777216 | bytes 4194304 | tf_op jit(solution)/shard_map/nk,cmjk->cmjn/dot_general | solution.py:44
  138.1 70.2 %all-to-all-done.1 = f32[12,256,4,128]{3,2,0,1:T(4,128)} async-done(((f32[12,256,4,128]{3,2,0,1:T(4,128)}), f32[12,256,4,128]{3,2,0,1:T(4,128)}, u32[]{:S(2)}, u32[]{:S(2)}) %all-to-all-start.1) | async-done | bytes 6291488 | tf_op jit(solution)/shard_map/all_to_all | solution.py:49
  208.3 5.0 copy.38
  213.2 144.5 %fusion = f32[12,32,4,1024]{3,1,2,0:T(8,128)S(1)} fusion(f32[12,4,8,4,8,128]{5,4,3,2,1,0:T(8,128)S(1)} %bitcast.70, f32[1024,1024,1,1]{1,0,3,2:T(8,128)S(1)} %copy-done.2), kind=kOutput, calls=%fused_computation | convolution fusion | flops 19327352832 | bytes 16777216 | tf_op jit(solution)/shard_map/nk,cmjk->cmjn/dot_general | solution.py:44
  357.8 0.8 slice_reduce_fusion.2
  358.6 1.3 multiply_add_fusion.1
  360.0 0.2 fusion.110
  360.2 29.0 %fusion.14 = f32[6,32,4,1024]{3,1,2,0:T(8,128)S(1)} fusion(f32[6,32,4,1024]{3,1,2,0:T(8,128)S(1)} %fusion.110), kind=kOutput, calls=%fused_computation.17 | convolution fusion | flops 9680453632 | bytes 6291456 | tf_op jit(solution)/shard_map/nk,cmjk->cmjn/dot_general | solution.py:44
  389.2 9.1 %copy.40 = f32[6,32,4,1024]{1,2,0,3:T(4,128)} copy(f32[6,32,4,1024]{3,1,2,0:T(8,128)S(1)} %fusion.14) | data formatting | bytes 6291456 | tf_op jit(solution)/shard_map/nk,cmjk->cmjn/dot_general | solution.py:44
  398.3 12.3 %reshape.77 = f32[8,1,98304]{2,1,0:T(1,128)} reshape(f32[1024,6,4,32]{3,2,1,0:T(4,128)} %bitcast.63) | data formatting | bytes 6291456
  410.6 41.0 %all_to_all.73 = f32[8,1,98304]{2,1,0:T(1,128)S(1)} all-to-all(f32[8,1,98304]{2,1,0:T(1,128)} %reshape.77), channel_id=1, replica_groups=mesh['ax'=8,'az'=16] {'ax'}, dimensions={0} | all-to-all | bytes 6291456 | tf_op jit(solution)/shard_map/all_to_all | solution.py:63
  451.6 0.5 broadcast.149
  452.1 11.1 %reduce = f32[8,98304]{1,0:T(8,128)} reduce(f32[8,1,98304]{2,1,0:T(1,128)S(1)} %all_to_all.73, f32[]{:T(128)} %broadcast.149), dimensions={1}, to_apply=%all_to_all.60.reduce_sub_computation | reduce | bytes 6291460 | tf_op jit(solution)/shard_map/all_to_all | solution.py:63
  463.2 13.3 %reshape.78 = f32[1024,6,4,32]{3,2,1,0:T(4,128)} reshape(f32[8,98304]{1,0:T(8,128)} %reduce) | data formatting | bytes 6291456
  476.5 11.4 %copy.56 = f32[6,32,4,8,128]{4,1,3,2,0:T(8,128)} copy(f32[6,32,4,8,128]{1,2,0,4,3:T(4,128)} %bitcast.64) | data formatting | bytes 6291456 | tf_op jit(solution)/shard_map/all_to_all | solution.py:63
  487.9 7.9 %convolution_bitcast_fusion.2 = f32[6,256,4,128]{1,3,2,0:T(8,128)S(1)} fusion(f32[6,256,4,128]{3,1,2,0:T(8,128)} %bitcast.69), kind=kOutput, calls=%fused_computation.30 | convolution fusion | flops 2416967680 | bytes 6291456 | tf_op jit(solution)/shard_map/nm,cmjk->cnjk/dot_general | solution.py:41
  495.8 3.0 copy.44
  498.8 6.7 %all-to-all-start.3 = ((f32[6,256,4,128]{3,2,0,1:T(4,128)}), f32[6,256,4,128]{3,2,0,1:T(4,128)S(1)}, u32[]{:S(2)}, u32[]{:S(2)}) async-start(f32[6,256,4,128]{3,2,0,1:T(4,128)} %copy.44), calls=%async_computation.3 | async-start | bytes 6291456 | tf_op jit(solution)/shard_map/all_to_all | solution.py:68
  505.5 0.1 broadcast_add_fusion
  505.6 1.0 multiply_add_fusion.2
  506.6 41.4 %all-to-all-done.3 = f32[6,256,4,128]{3,2,0,1:T(4,128)S(1)} async-done(((f32[6,256,4,128]{3,2,0,1:T(4,128)}), f32[6,256,4,128]{3,2,0,1:T(4,128)S(1)}, u32[]{:S(2)}, u32[]{:S(2)}) %all-to-all-start.3) | async-done | bytes 3145760 | tf_op jit(solution)/shard_map/all_to_all | solution.py:68
  548.0 0.6 copy.45
  548.6 2.0 copy.46
  550.7 3.3 convolution_bitcast_fusion.1
  554.0 2.5 fusion.27
  (14 shorter events, 0.1 us)
Async XLA Ops:
  115.4 92.9 %all-to-all-start.1 = ((f32[12,256,4,128]{3,2,0,1:T(4,128)}), f32[12,256,4,128]{3,2,0,1:T(4,128)}, u32[]{:S(2)}, u32[]{:S(2)}) async-start(f32[12,256,4,128]{3,2,0,1:T(4,128)} %copy.37), calls=%async_computation.1 | async-start | bytes 12582912 | tf_op jit(solution)/shard_map/all_to_all | solution.py:49
  208.3 5.0 copy-start.2
  498.8 6.7 %copy-start.4 = (f32[64]{0:T(128)S(1)}, f32[64]{0:T(128)}, u32[]{:S(2)}) copy-start(f32[64]{0:T(128)} %param.9) | copy-start | bytes 772
  498.8 49.2 %all-to-all-start.3 = ((f32[6,256,4,128]{3,2,0,1:T(4,128)}), f32[6,256,4,128]{3,2,0,1:T(4,128)S(1)}, u32[]{:S(2)}, u32[]{:S(2)}) async-start(f32[6,256,4,128]{3,2,0,1:T(4,128)} %copy.44), calls=%async_computation.3 | async-start | bytes 6291456 | tf_op jit(solution)/shard_map/all_to_all | solution.py:68
  550.6 3.3 copy-start
  550.6 3.3 copy-start.1
  550.7 3.3 copy-start.3
where the time goes:
time: 563 us; the launch traced here: 557 us
  matrix products  207 us (37%)
  blocking collectives  121 us (21%)
  waiting for transfers between devices  112 us (20%)
  local copies, waits for them, and re-layouts  69.6 us (12%)
  other arithmetic  34.8 us (6%)
  starting transfers between devices  11.7 us (2%)
    dot_general x2, matrix products, along_axial(): jnp.einsum('nk,cmjk->cmjn', axial_table, field, precision=lax.Precision.H...  174 us
    all_to_all x1, blocking collectives, body(): lax.all_to_all(grid, 'az', split_axis=2, concat_axis=1, tiled=True)  79.9 us
    all_to_all x1, waiting for transfers between devices, body(): lax.all_to_all(halfway, 'ax', split_axis=1, concat_axis=3, tiled=True)  70.2 us
    all_to_all x1, waiting for transfers between devices, body(): lax.all_to_all(turned, 'az', split_axis=1, concat_axis=2, tiled=True)  41.4 us
    all_to_all x1, blocking collectives, body(): lax.all_to_all(partial_field, 'ax', split_axis=3, concat_axis=1, tiled=True)  41 us
    unnamed x12, local copies, waits for them, and re-layouts  25.6 us
    dot_general x2, matrix products, along_azimuth(): jnp.einsum('nm,cmjk->cnjk', azimuth_table, field, precision=lax.Precision...  22.2 us
    dot_general x2, other arithmetic, along_axial(): jnp.einsum('nk,cmjk->cmjn', axial_table, field, precision=lax.Precision.H...  17.9 us
  transfers between devices with their start and end apart: 2, of which 2 were waited for; matrix products, arithmetic and copies ran while one was open for 3% of the time, Pallas kernels for 0%

commit v1 on v0

--- a/solution.py
+++ b/solution.py
@@ -60,7 +60,12 @@
     products = jnp.concatenate((tangent_rhs, second_rhs), axis=0)
     partial_field = along_axial(products)
     turned = along_azimuth(
-        lax.all_to_all(partial_field, "ax", split_axis=3, concat_axis=1, tiled=True)
+        jnp.concatenate(
+            lax.all_to_all(
+                jnp.stack(jnp.split(partial_field, lax.axis_size("ax"), axis=3)), "ax", 0, 0
+            ),
+            axis=1,
+        )
     )
     spectral = jnp.einsum(
         "jr,cmjk->cmrk",

time: 563 us -> 504 us (0.90)
  local copies, waits for them, and re-layouts: 69.6 us -> 23.9 us
  other arithmetic: 34.8 us -> 23.7 us
    unnamed x12 -> x17, local copies, waits for them, and re-layouts: 25.6 us -> 0.4 us
    all_to_all x2 -> x0, local copies, waits for them, and re-layouts: 11.9 us -> none  [body(): lax.all_to_all(partial_field, 'ax', split_axis=3, concat_axis=1, tiled=True)]
    all_to_all x1 -> x0, other arithmetic: 11.1 us -> none  [body(): lax.all_to_all(partial_field, 'ax', split_axis=3, concat_axis=1, tiled=True)]
    dot_general x1 -> x0, local copies, waits for them, and re-layouts: 9.06 us -> none  [along_axial(): jnp.einsum('nk,cmjk->cmjn', axial_table, field, precision=lax.Precision.H...]
  transfers between devices with their start and end apart: 2 -> 2, of which waited for: 2 -> 2; matrix products, arithmetic and copies ran while one was open for 3% -> 4% of each run, Pallas kernels for 0% -> 0%
where the time goes in v1:
time: 504 us; the launch traced here: 498 us
  matrix products  206 us (41%)
  blocking collectives  121 us (24%)
  waiting for transfers between devices  112 us (22%)
  local copies, waits for them, and re-layouts  23.9 us (5%)
  other arithmetic  23.7 us (5%)
  starting transfers between devices  11.7 us (2%)
    dot_general x2, matrix products, along_axial(): jnp.einsum('nk,cmjk->cmjn', axial_table, field, precision=lax.Precision.H...  174 us
    all_to_all x1, blocking collectives, body(): lax.all_to_all(grid, 'az', split_axis=2, concat_axis=1, tiled=True)  79.9 us
    all_to_all x1, waiting for transfers between devices, body(): lax.all_to_all(halfway, 'ax', split_axis=1, concat_axis=3, tiled=True)  70.1 us
    all_to_all x1, waiting for transfers between devices, body(): lax.all_to_all(turned, 'az', split_axis=1, concat_axis=2, tiled=True)  41.4 us
    all_to_all x1, blocking collectives, body(): lax.all_to_all(jnp.stack(jnp.split(partial_field, lax.axis_size('ax'), ax...  41 us
    dot_general x2, matrix products, along_azimuth(): jnp.einsum('nm,cmjk->cnjk', azimuth_table, field, precision=lax.Precision...  20.6 us
    dot_general x2, other arithmetic, along_axial(): jnp.einsum('nk,cmjk->cmjn', axial_table, field, precision=lax.Precision.H...  17.9 us
    transpose x2, local copies, waits for them, and re-layouts, along_azimuth(): jnp.einsum('nm,cmjk->cnjk', azimuth_table, field, precision=lax.Precision...  10.9 us
  transfers between devices with their start and end apart: 2, of which 2 were waited for; matrix products, arithmetic and copies ran while one was open for 4% of the time, Pallas kernels for 0%

profile of v1, /device:TPU:3, one launch (start us, length us, event | category | flops | bytes accessed | tf_op | source)
XLA Modules:
  0.0 498.5 jit_solution(4703808990904978728)
XLA Ops:
  0.7 8.1 %fusion.23 = f32[12,16,64,128]{3,2,1,0:T(8,128)S(1)} fusion(f32[3,16,64,128]{3,2,1,0:T(8,128)} %param.8, f32[3,16,64,128]{3,2,1,0:T(8,128)} %param.7, f32[3,16,64,128]{3,2,1,0:T(8,128)} %param.6, f32[3,16,64,128]{3,2,1,0:T(8,128)} %param.5, f32[64]{0:T(128)S(1)} %compare_select_fusion, s32[64]{0:T(128)S(1)} %multiply_add_fusion.3), kind=kOutput, calls=%fused_computation.27 | convolution fusion | flops 1212739584 | bytes 12583424 | tf_op jit(solution)/shard_map/jr,cmrk->cmjk/dot_general | solution.py:47
  8.8 3.6 copy.32
  12.4 79.9 %all_to_all.59 = f32[12,16,64,128]{3,1,0,2:T(8,128)S(1)} all-to-all(f32[12,16,64,128]{3,1,0,2:T(8,128)S(1)} %copy.32), channel_id=1, replica_groups=mesh['ax'=8,'az'=16] {'az'}, dimensions={2} | all-to-all | bytes 12582912 | tf_op jit(solution)/shard_map/all_to_all | solution.py:48
  92.4 0.9 copy.34
  93.2 14.4 %convolution_bitcast_fusion = f32[12,256,4,128]{1,3,2,0:T(8,128)} fusion(f32[12,256,4,128]{3,1,2,0:T(8,128)S(1)} %bitcast.91), kind=kOutput, calls=%fused_computation.28 | convolution fusion | flops 4832886784 | bytes 12582912 | tf_op jit(solution)/shard_map/nm,cmjk->cnjk/dot_general | solution.py:41
  107.6 8.0 %copy.36 = f32[12,256,4,128]{3,2,0,1:T(4,128)} copy(f32[12,256,4,128]{1,3,2,0:T(8,128)} %convolution_bitcast_fusion) | data formatting | bytes 12582912 | tf_op jit(solution)/shard_map/nm,cmjk->cnjk/transpose | solution.py:41
  115.6 5.1 %all-to-all-start.1 = ((f32[12,256,4,128]{3,2,0,1:T(4,128)}), f32[12,256,4,128]{3,2,0,1:T(4,128)}, u32[]{:S(2)}, u32[]{:S(2)}) async-start(f32[12,256,4,128]{3,2,0,1:T(4,128)} %copy.36), calls=%async_computation.1 | async-start | bytes 12582912 | tf_op jit(solution)/shard_map/all_to_all | solution.py:49
  120.7 17.7 %fusion.116 = f32[1024,1024,1,1]{1,0,3,2:T(8,128)} fusion(), kind=kLoop, calls=%fused_computation.19.clone.1 | loop fusion | flops 16777216 | bytes 4194304 | tf_op jit(solution)/shard_map/nk,cmjk->cmjn/dot_general | solution.py:44
  138.4 70.1 %all-to-all-done.1 = f32[12,256,4,128]{3,2,0,1:T(4,128)} async-done(((f32[12,256,4,128]{3,2,0,1:T(4,128)}), f32[12,256,4,128]{3,2,0,1:T(4,128)}, u32[]{:S(2)}, u32[]{:S(2)}) %all-to-all-start.1) | async-done | bytes 6291488 | tf_op jit(solution)/shard_map/all_to_all | solution.py:49
  208.5 5.0 copy.37
  213.5 144.5 %fusion = f32[12,32,4,1024]{3,1,2,0:T(8,128)S(1)} fusion(f32[12,4,8,4,8,128]{5,4,3,2,1,0:T(8,128)S(1)} %bitcast.96, f32[1024,1024,1,1]{1,0,3,2:T(8,128)S(1)} %copy-done.2), kind=kOutput, calls=%fused_computation | convolution fusion | flops 19327352832 | bytes 16777216 | tf_op jit(solution)/shard_map/nk,cmjk->cmjn/dot_general | solution.py:44
  358.0 0.8 slice_reduce_fusion.2
  358.8 1.3 multiply_add_fusion.1
  360.2 0.2 fusion.118
  360.4 29.1 %fusion.14 = f32[6,32,4,1024]{3,1,2,0:T(8,128)S(1)} fusion(f32[6,32,4,1024]{3,1,2,0:T(8,128)S(1)} %fusion.118), kind=kOutput, calls=%fused_computation.17 | convolution fusion | flops 9680453632 | bytes 6291456 | tf_op jit(solution)/shard_map/nk,cmjk->cmjn/dot_general | solution.py:44
  389.5 0.1 fusion.37
  389.6 0.1 fusion.36
  389.7 0.1 fusion.35
  389.9 0.1 fusion.31
  390.0 0.1 fusion.30
  390.0 41.0 %all_to_all.60 = f32[8,6,32,4,128]{4,2,3,1,0:T(8,128)S(1)} all-to-all(f32[8,6,32,4,128]{4,2,3,1,0:T(8,128)S(1)} %fusion.30), channel_id=1, replica_groups=mesh['ax'=8,'az'=16] {'ax'}, dimensions={0} | all-to-all | bytes 6291456 | tf_op jit(solution)/shard_map/all_to_all | solution.py:64
  431.0 0.4 copy.39
  431.5 6.3 %convolution_bitcast_fusion.2 = f32[6,256,4,128]{1,3,2,0:T(8,128)S(1)} fusion(f32[6,256,4,128]{3,1,2,0:T(8,128)S(1)} %bitcast.93), kind=kOutput, calls=%fused_computation.30 | convolution fusion | flops 2416967680 | bytes 6291456 | tf_op jit(solution)/shard_map/nm,cmjk->cnjk/dot_general | solution.py:41
  437.8 2.9 copy.41
  440.7 6.7 %all-to-all-start.3 = ((f32[6,256,4,128]{3,2,0,1:T(4,128)}), f32[6,256,4,128]{3,2,0,1:T(4,128)S(1)}, u32[]{:S(2)}, u32[]{:S(2)}) async-start(f32[6,256,4,128]{3,2,0,1:T(4,128)} %copy.41), calls=%async_computation.3 | async-start | bytes 6291456 | tf_op jit(solution)/shard_map/all_to_all | solution.py:73
  447.4 0.1 broadcast_add_fusion
  447.4 1.0 multiply_add_fusion.2
  448.4 41.4 %all-to-all-done.3 = f32[6,256,4,128]{3,2,0,1:T(4,128)S(1)} async-done(((f32[6,256,4,128]{3,2,0,1:T(4,128)}), f32[6,256,4,128]{3,2,0,1:T(4,128)S(1)}, u32[]{:S(2)}, u32[]{:S(2)}) %all-to-all-start.3) | async-done | bytes 3145760 | tf_op jit(solution)/shard_map/all_to_all | solution.py:73
  489.8 0.6 copy.42
  490.4 2.0 copy.43
  492.5 3.3 convolution_bitcast_fusion.1
  495.8 2.5 fusion.27
  (17 shorter events, 0.2 us)
Async XLA Ops:
  115.6 92.9 %all-to-all-start.1 = ((f32[12,256,4,128]{3,2,0,1:T(4,128)}), f32[12,256,4,128]{3,2,0,1:T(4,128)}, u32[]{:S(2)}, u32[]{:S(2)}) async-start(f32[12,256,4,128]{3,2,0,1:T(4,128)} %copy.36), calls=%async_computation.1 | async-start | bytes 12582912 | tf_op jit(solution)/shard_map/all_to_all | solution.py:49
  208.5 5.0 copy-start.2
  440.7 6.7 %copy-start.4 = (f32[64]{0:T(128)S(1)}, f32[64]{0:T(128)}, u32[]{:S(2)}) copy-start(f32[64]{0:T(128)} %param.9) | copy-start | bytes 772
  440.7 49.2 %all-to-all-start.3 = ((f32[6,256,4,128]{3,2,0,1:T(4,128)}), f32[6,256,4,128]{3,2,0,1:T(4,128)S(1)}, u32[]{:S(2)}, u32[]{:S(2)}) async-start(f32[6,256,4,128]{3,2,0,1:T(4,128)} %copy.41), calls=%async_computation.3 | async-start | bytes 6291456 | tf_op jit(solution)/shard_map/all_to_all | solution.py:73
  492.5 3.3 copy-start
  492.5 3.3 copy-start.1
  492.5 3.3 copy-start.3
